TPU v7x, 32 devices: a whole 2x2x4 slice. The times are simulated.
32 devices in a mesh: row: 2 (over y), col: 4 (over x, core), tm: 4 (over z).
Axes of the slice: x: 2, y: 2, z: 4, core: 2. Of those that a mesh axis runs over, the one named last changes fastest.
Arguments:
- filled_orbitals: bfloat16 [4, 1024, 1024], P('col', 'row', 'tm'), may hold values from -0.1875 to 0.1875
- empty_orbitals: bfloat16 [4, 1024, 3072], P('col', 'row', 'tm'), may hold values from -0.109375 to 0.109375
- filled_depth: bfloat16 [1024], P('tm'), may hold values from 0.019897461 to 2
- empty_depth: bfloat16 [3072], P('tm'), may hold values from 0.019897461 to 2
- time_points: float32 [4], P('tm'), may hold values from 0.05 to 8
- cosine_weights: float32 [4, 4], replicated, may hold values from -3 to 3
Outputs:
- polar_freq: float32 [4, 4, 1024, 4096], P(None, None, ('row', 'tm'), 'col')
All inputs are finite; a program needn't handle non-finite values.
Results may differ from a plain program's by a relative error of at most 0.0033.
Values may be sent and summed in bfloat16 or wider, within the bound.
No kernel may reach another device: no remote copies, remote signals or barrier semaphores. Data moves between devices by JAX's collectives and lax.ppermute only.
A program may use at most 128 MiB of HBM per device.

v0:
```python
import jax
import jax.numpy as jnp
from jax import lax
from jax.sharding import PartitionSpec as P


def tile_product(left_points, right_points, depths, tau_value):
    band_count = left_points.shape[-1]
    weight_row = jnp.exp(-depths.astype(jnp.float32) * tau_value)
    scaled = (
        right_points.reshape(-1, band_count).astype(jnp.float32) * weight_row[None, :]
    ).astype(jnp.bfloat16)
    return lax.dot_general(
        left_points.reshape(-1, band_count),
        scaled,
        (((1,), (1,)), ((), ())),
        preferred_element_type=jnp.float32,
    )


def on_device(
    filled_orbitals, empty_orbitals, filled_depth, empty_depth, time_points, cosine_weights
):
    tau_value = time_points[0]
    filled_bands, empty_bands, filled_all, empty_all = (
        lax.all_gather(filled_orbitals, "tm", axis=2, tiled=True),
        lax.all_gather(empty_orbitals, "tm", axis=2, tiled=True),
        lax.all_gather(filled_depth, "tm", axis=0, tiled=True),
        lax.all_gather(empty_depth, "tm", axis=0, tiled=True),
    )
    filled_rows, empty_rows = (
        lax.all_gather(filled_bands, "col", axis=0, tiled=True),
        lax.all_gather(empty_bands, "col", axis=0, tiled=True),
    )
    column_filled, column_empty = lax.all_gather(
        (filled_bands, empty_bands), "row", axis=1, tiled=True
    )
    green_filled = tile_product(filled_rows, column_filled, filled_all, tau_value)
    green_empty = tile_product(empty_rows, column_empty, empty_all, tau_value)
    polar_time = (
        (-(green_filled * green_empty))
        .astype(jnp.bfloat16)
        .reshape(filled_rows.shape[0], filled_rows.shape[1], -1)
    )
    return jnp.einsum(
        "ft,tabc->fabc",
        cosine_weights,
        lax.all_to_all(polar_time[None], "tm", split_axis=2, concat_axis=0, tiled=True).astype(
            jnp.float32
        ),
        precision=lax.Precision.HIGHEST,
    )


def solution(mesh):
    in_specs = (P("col", "row", "tm"), P("col", "row", "tm"), P("tm"), P("tm"), P("tm"), P())
    out_specs = P(None, None, ("row", "tm"), "col")
    return jax.shard_map(
        on_device, mesh=mesh, in_specs=in_specs, out_specs=out_specs, check_vma=False
    )
```

profile of v0, /device:TPU:0, one launch (start us, length us, event | category | flops | bytes accessed | tf_op | source)
XLA Modules:
  0.0 491.7 jit_solution(13205183618008928850)
XLA Ops:
  6.5 0.7 all-gather.15.cloned.1.call-update
  7.3 0.0 all-gather.9.cloned.1.call-start
  7.3 0.7 all-gather.9.cloned.1.call-update
  8.0 0.0 all-gather.17.cloned.1.call-start
  8.1 67.0 %all-gather.15.cloned.1.call-done = bf16[1,512,3072]{2,1,0:T(8,128)(2,1)} async-done(((bf16[1,512,768]{2,1,0:T(8,128)(2,1)}), bf16[1,512,3072]{2,1,0:T(8,128)(2,1)}) %all-gather.15.cloned.1.call-update) | async-done | bytes 3145744 | tf_op jit(solution)/shard_map/all_gather | solution.py:27
  75.1 0.0 all-gather.19.cloned.1.call-start
  75.2 0.5 all-gather.19.cloned.1.call-update
  75.7 0.0 all-gather.11.cloned.1.call-start
  75.8 29.5 %all-gather.9.cloned.1.call-done = bf16[1,512,1024]{2,1,0:T(8,128)(2,1)} async-done(((bf16[1,512,256]{2,1,0:T(8,128)(2,1)}), bf16[1,512,1024]{2,1,0:T(8,128)(2,1)}) %all-gather.9.cloned.1.call-update) | async-done | bytes 1048592 | tf_op jit(solution)/shard_map/all_gather | solution.py:26
  105.3 0.0 all-gather.13.cloned.1.call-start
  105.3 0.5 all-gather.13.cloned.1.call-update
  106.6 10.1 %all-gather = bf16[4,1,256]{2,1,0:T(2,128)(2,1)S(1)} all-gather(bf16[1,1,256]{2,1,0:T(2,128)(2,1)S(1)} %reshape.26), channel_id=1, replica_groups=mesh['row'=2,'col'=4,'tm'=4] {'tm'}, dimensions={0}, use_global_device_ids=true | all-gather | bytes 2560 | tf_op jit(solution)/shard_map/all_gather | solution.py:28
  116.7 13.1 %all-gather.1 = bf16[4,1,768]{2,1,0:T(2,128)(2,1)S(1)} all-gather(bf16[1,1,768]{2,1,0:T(2,128)(2,1)S(1)} %reshape.28), channel_id=1, replica_groups=mesh['row'=2,'col'=4,'tm'=4] {'tm'}, dimensions={0}, use_global_device_ids=true | all-gather | bytes 7680 | tf_op jit(solution)/shard_map/all_gather | solution.py:29
  129.8 55.7 %all-gather.17.cloned.1.call-done = bf16[1,1024,3072]{2,1,0:T(8,128)(2,1)} async-done(((bf16[1,512,3072]{2,1,0:T(8,128)(2,1)}), bf16[1,1024,3072]{2,1,0:T(8,128)(2,1)}) %all-gather.17.cloned.1.call-update) | async-done | bytes 6291472 | tf_op jit(solution)/shard_map/all_gather | solution.py:35
  185.5 83.5 %all-gather.19.cloned.1.call-done = bf16[4,512,3072]{2,1,0:T(8,128)(2,1)} async-done(((bf16[1,512,3072]{2,1,0:T(8,128)(2,1)}), bf16[4,512,3072]{2,1,0:T(8,128)(2,1)}) %all-gather.19.cloned.1.call-update) | async-done | bytes 12582928 | tf_op jit(solution)/shard_map/all_gather | solution.py:33
  269.0 18.9 %fusion.1 = f32[1024,2048]{1,0:T(8,128)} fusion(bf16[2048,3072]{1,0:T(8,128)(2,1)} %bitcast.35, bf16[1,1024,3072]{2,1,0:T(8,128)(2,1)} %all-gather.17.cloned.1.call-done, f32[3072]{0:T(1024)S(1)} %bitcast.33), kind=kOutput, calls=%fused_computation.3 | convolution fusion | flops 12894339072 | bytes 27275264 | tf_op jit(solution)/shard_map/dot_general | solution.py:13
  287.9 15.6 %all-gather.11.cloned.1.call-done = bf16[1,1024,1024]{2,1,0:T(8,128)(2,1)} async-done(((bf16[1,512,1024]{2,1,0:T(8,128)(2,1)}), bf16[1,1024,1024]{2,1,0:T(8,128)(2,1)}) %all-gather.11.cloned.1.call-update) | async-done | bytes 2097168 | tf_op jit(solution)/shard_map/all_gather | solution.py:35
  303.5 35.9 %all-gather.13.cloned.1.call-done = bf16[4,512,1024]{2,1,0:T(8,128)(2,1)} async-done(((bf16[1,512,1024]{2,1,0:T(8,128)(2,1)}), bf16[4,512,1024]{2,1,0:T(8,128)(2,1)}) %all-gather.13.cloned.1.call-update) | async-done | bytes 4194320 | tf_op jit(solution)/shard_map/all_gather | solution.py:32
  339.4 11.8 %fusion.6 = bf16[2048,1024]{0,1:T(8,128)(2,1)} fusion(f32[1024,2048]{1,0:T(8,128)} %fusion.1, bf16[2048,1024]{1,0:T(8,128)(2,1)} %bitcast.36, bf16[1,1024,1024]{2,1,0:T(8,128)(2,1)} %all-gather.11.cloned.1.call-done, f32[1024]{0:T(1024)S(1)} %bitcast.34), kind=kOutput, calls=%fused_computation.9 | convolution fusion | flops 4304404480 | bytes 18878464 | tf_op jit(solution)/shard_map/dot_general | solution.py:13
  351.2 7.8 %broadcast_in_dim_reshape.3 = bf16[1,4,512,1024]{2,1,3,0:T(4,128)(2,1)} reshape(bf16[2048,1024]{0,1:T(8,128)(2,1)} %fusion.6) | data formatting | bytes 8388608 | tf_op jit(solution)/shard_map/broadcast_in_dim;reshape | solution.py:48
  359.0 10.0 %copy.11 = bf16[1,4,512,1024]{3,1,0,2:T(4,128)(2,1)} copy(bf16[1,4,512,1024]{2,1,3,0:T(4,128)(2,1)} %broadcast_in_dim_reshape.3) | data formatting | bytes 8388608 | tf_op jit(solution)/shard_map/broadcast_in_dim;reshape | solution.py:48
  369.0 98.1 %all_to_all.18 = bf16[1,4,512,1024]{3,1,0,2:T(4,128)(2,1)S(1)} all-to-all(bf16[1,4,512,1024]{3,1,0,2:T(4,128)(2,1)} %copy.11), channel_id=1, replica_groups=mesh['row'=2,'col'=4,'tm'=4] {'tm'}, dimensions={2} | all-to-all | bytes 8388608 | tf_op jit(solution)/shard_map/all_to_all | solution.py:48
  467.2 9.4 %convolution_bitcast_fusion = f32[4,4,128,1024]{3,0,2,1:T(4,128)S(1)} fusion(bf16[1,4,4,128,1024]{4,1,3,2,0:T(4,128)(2,1)S(1)} %bitcast.32, f32[4,4]{1,0:T(4,128)S(1)} %copy-done), kind=kOutput, calls=%fused_computation.5 | convolution fusion | flops 100663296 | bytes 12582976 | tf_op jit(solution)/shard_map/ft,tabc->fabc/dot_general | solution.py:45
  476.6 8.3 %copy.14 = f32[4,4,128,1024]{3,2,1,0:T(8,128)} copy(f32[4,4,128,1024]{3,0,2,1:T(4,128)S(1)} %convolution_bitcast_fusion) | data formatting | bytes 16777216 | tf_op jit(solution)/shard_map/ft,tabc->fabc/dot_general | solution.py:45
  (13 shorter events, 0.1 us)
Async XLA Ops:
  6.5 460.6 %copy-start = (f32[4,4]{1,0:T(4,128)S(1)}, f32[4,4]{1,0:T(4,128)}, u32[]{:S(2)}) copy-start(f32[4,4]{1,0:T(4,128)} %param.11) | copy-start | bytes 196
  6.5 68.6 %all-gather.15.cloned.1.call-start = ((), (), s32[]{:S(2)}) async-start(), calls=%async_computation.4 | async-start | bytes 3932160 | tf_op jit(solution)/shard_map/all_gather | solution.py:27
  7.3 98.0 %all-gather.9.cloned.1.call-start = ((), (), s32[]{:S(2)}) async-start(), calls=%async_computation.1 | async-start | bytes 1310720 | tf_op jit(solution)/shard_map/all_gather | solution.py:26
  8.0 177.5 %all-gather.17.cloned.1.call-start = ((), (), s32[]{:S(2)}) async-start(), calls=%async_computation.5 | async-start | bytes 9437184 | tf_op jit(solution)/shard_map/all_gather | solution.py:35
  75.1 31.4 %copy-start.1 = (bf16[768]{0:T(1024)(128)(2,1)S(1)}, bf16[768]{0:T(1024)(128)(2,1)}, u32[]{:S(2)}) copy-start(bf16[768]{0:T(1024)(128)(2,1)} %param.9) | copy-start | bytes 4612
  75.1 31.4 %copy-start.2 = (bf16[256]{0:T(256)(128)(2,1)S(1)}, bf16[256]{0:T(256)(128)(2,1)}, u32[]{:S(2)}) copy-start(bf16[256]{0:T(256)(128)(2,1)} %param.8) | copy-start | bytes 1540
  75.1 193.9 %all-gather.19.cloned.1.call-start = ((), (), s32[]{:S(2)}) async-start(), calls=%async_computation.6 | async-start | bytes 15728640 | tf_op jit(solution)/shard_map/all_gather | solution.py:33
  75.7 227.8 %all-gather.11.cloned.1.call-start = ((), (), s32[]{:S(2)}) async-start(), calls=%async_computation.2 | async-start | bytes 3145728 | tf_op jit(solution)/shard_map/all_gather | solution.py:35
  105.3 234.2 %all-gather.13.cloned.1.call-start = ((), (), s32[]{:S(2)}) async-start(), calls=%async_computation.3 | async-start | bytes 5242880 | tf_op jit(solution)/shard_map/all_gather | solution.py:32
Sparse Core Ops, SparseCore 0:
  8.9 66.1 all-gather.14
  76.7 28.5 all-gather.8
  106.8 78.6 all-gather.16
  186.9 82.0 all-gather.18
  270.4 33.0 all-gather.10
  305.0 34.4 all-gather.12
where the time goes:
time: 492 us
  waiting for transfers between devices  290 us (59%)
  blocking collectives  121 us (25%)
  matrix products  40.1 us (8%)
  local copies, waits for them, and re-layouts  26.1 us (5%)
  between operations  14.2 us (3%)
    all_to_all x1, blocking collectives, on_device(): lax.all_to_all(polar_time[None], 'tm', split_axis=2, concat_axis=0, tiled...  98.1 us
    all_gather x1, waiting for transfers between devices, on_device(): lax.all_gather(empty_bands, 'col', axis=0, tiled=True)  83.5 us
    all_gather x2, waiting for transfers between devices, on_device(): lax.all_gather((filled_bands, empty_bands), 'row', axis=1, tiled=True)  71.3 us
    all_gather x1, waiting for transfers between devices, on_device(): lax.all_gather(empty_orbitals, 'tm', axis=2, tiled=True)  67 us
    all_gather x1, waiting for transfers between devices, on_device(): lax.all_gather(filled_bands, 'col', axis=0, tiled=True)  35.9 us
    dot_general x2, matrix products, tile_product(): lax.dot_general(left_points.reshape(-1, band_count), scaled, (((1,), (1,)...  30.6 us
    all_gather x1, waiting for transfers between devices, on_device(): lax.all_gather(filled_orbitals, 'tm', axis=2, tiled=True)  29.5 us
    another operation x2, local copies, waits for them, and re-layouts, on_device(): polar_time[None]  17.8 us
  transfers between devices with their start and end apart: 6, of which 6 were waited for; matrix products, arithmetic and copies ran while one was open for 4% of the time, Pallas kernels for 0%

commit v1 on v0

--- a/solution.py
+++ b/solution.py
@@ -2,6 +2,19 @@
 import jax.numpy as jnp
 from jax import lax
 from jax.sharding import PartitionSpec as P
+
+
+def gather_around(array, axis, dim):
+    ways = lax.axis_size(axis)
+    up = [(d, (d + 1) % ways) for d in range(ways)]
+    down = [(d, (d - 1) % ways) for d in range(ways)]
+    earlier, later = ([array], [array])
+    for _ in range(ways // 2):
+        earlier.append(lax.ppermute(earlier[-1], axis, up))
+    for _ in range((ways - 1) // 2):
+        later.append(lax.ppermute(later[-1], axis, down))
+    line = jnp.concatenate([*earlier[::-1], *later[1:]], axis=dim)
+    return jnp.roll(line, (lax.axis_index(axis) - ways // 2) * array.shape[dim], axis=dim)
 
 
 def tile_product(left_points, right_points, depths, tau_value):
@@ -29,7 +42,7 @@
         lax.all_gather(empty_depth, "tm", axis=0, tiled=True),
     )
     filled_rows, empty_rows = (
-        lax.all_gather(filled_bands, "col", axis=0, tiled=True),
+        gather_around(filled_bands, "col", 0),
         lax.all_gather(empty_bands, "col", axis=0, tiled=True),
     )
     column_filled, column_empty = lax.all_gather(

time: 492 us -> 439 us (0.89)
  waiting for transfers between devices: 290 us -> 244 us
  local copies, waits for them, and re-layouts: 26.1 us -> 19.6 us
    all_gather x1 -> x0, waiting for transfers between devices: 35.9 us -> none  [on_device(): lax.all_gather(filled_bands, 'col', axis=0, tiled=True)]
    all_gather x2, waiting for transfers between devices: 71.3 us -> 47.1 us  [on_device(): lax.all_gather((filled_bands, empty_bands), 'row', axis=1, tiled=True)]
    another operation x2 -> x1, local copies, waits for them, and re-layouts: 17.8 us -> 3.24 us  [on_device(): polar_time[None]]
    ppermute x0 -> x3, waiting for transfers between devices: none -> 14.4 us  [the longest x2 14.4 us: gather_around(): earlier.append(lax.ppermute(earlier[-1], axis, up))]
    unnamed x8 -> x13, local copies, waits for them, and re-layouts: 0.02 us -> 5.52 us
  transfers between devices with their start and end apart: 6 -> 8, of which waited for: 6 -> 6; matrix products, arithmetic and copies ran while one was open for 4% -> 6% of each run, Pallas kernels for 0% -> 0%
where the time goes in v1:
time: 439 us; the launch traced here: 438 us
  waiting for transfers between devices  244 us (56%)
  blocking collectives  121 us (28%)
  matrix products  38.6 us (9%)
  local copies, waits for them, and re-layouts  19.6 us (4%)
  between operations  13.9 us (3%)
    all_to_all x1, blocking collectives, on_device(): lax.all_to_all(polar_time[None], 'tm', split_axis=2, concat_axis=0, tiled...  97.4 us
    all_gather x1, waiting for transfers between devices, on_device(): lax.all_gather(empty_bands, 'col', axis=0, tiled=True)  83.5 us
    all_gather x1, waiting for transfers between devices, on_device(): lax.all_gather(empty_orbitals, 'tm', axis=2, tiled=True)  67 us
    all_gather x2, waiting for transfers between devices, on_device(): lax.all_gather((filled_bands, empty_bands), 'row', axis=1, tiled=True)  47.1 us
    all_gather x1, waiting for transfers between devices, on_device(): lax.all_gather(filled_orbitals, 'tm', axis=2, tiled=True)  29.5 us
    dot_general x2, matrix products, tile_product(): lax.dot_general(left_points.reshape(-1, band_count), scaled, (((1,), (1,)...  29.2 us
    ppermute x2, waiting for transfers between devices, gather_around(): earlier.append(lax.ppermute(earlier[-1], axis, up))  14.4 us
    all_gather x1, blocking collectives, on_device(): lax.all_gather(empty_depth, 'tm', axis=0, tiled=True)  13.1 us
  transfers between devices with their start and end apart: 8, of which 6 were waited for; matrix products, arithmetic and copies ran while one was open for 6% of the time, Pallas kernels for 0%

profile of v1, /device:TPU:0, one launch (start us, length us, event | category | flops | bytes accessed | tf_op | source)
XLA Modules:
  0.0 438.2 jit_solution(13781520922988406546)
XLA Ops:
  6.5 0.7 all-gather.12.cloned.1.call-update
  7.3 0.7 all-gather.8.cloned.1.call-update
  8.1 67.0 %all-gather.12.cloned.1.call-done = bf16[1,512,3072]{2,1,0:T(8,128)(2,1)} async-done(((bf16[1,512,768]{2,1,0:T(8,128)(2,1)}), bf16[1,512,3072]{2,1,0:T(8,128)(2,1)}) %all-gather.12.cloned.1.call-update) | async-done | bytes 3145744 | tf_op jit(solution)/shard_map/all_gather | solution.py:40
  75.2 0.5 all-gather.16.cloned.1.call-update
  75.7 29.5 %all-gather.8.cloned.1.call-done = bf16[1,512,1024]{2,1,0:T(8,128)(2,1)} async-done(((bf16[1,512,256]{2,1,0:T(8,128)(2,1)}), bf16[1,512,1024]{2,1,0:T(8,128)(2,1)}) %all-gather.8.cloned.1.call-update) | async-done | bytes 1048592 | tf_op jit(solution)/shard_map/all_gather | solution.py:39
  105.3 14.4 %collective-permute-done = bf16[1,512,1024]{2,1,0:T(8,128)(2,1)S(1)} collective-permute-done((bf16[1,512,1024]{2,1,0:T(8,128)(2,1)}, bf16[1,512,1024]{2,1,0:T(8,128)(2,1)S(1)}, u32[]{:S(2)}, u32[]{:S(2)}) %collective-permute-start) | collective-permute-done | bytes 1048608 | tf_op jit(solution)/shard_map/ppermute | solution.py:13
  119.7 1.7 collective-permute-start.2
  121.4 0.7 reshape.28
  122.8 0.7 reshape.26
  123.5 10.1 %all-gather = bf16[4,1,256]{2,1,0:T(2,128)(2,1)S(1)} all-gather(bf16[1,1,256]{2,1,0:T(2,128)(2,1)S(1)} %reshape.26), channel_id=1, replica_groups=mesh['row'=2,'col'=4,'tm'=4] {'tm'}, dimensions={0}, use_global_device_ids=true | all-gather | bytes 2560 | tf_op jit(solution)/shard_map/all_gather | solution.py:41
  133.6 13.1 %all-gather.1 = bf16[4,1,768]{2,1,0:T(2,128)(2,1)S(1)} all-gather(bf16[1,1,768]{2,1,0:T(2,128)(2,1)S(1)} %reshape.28), channel_id=1, replica_groups=mesh['row'=2,'col'=4,'tm'=4] {'tm'}, dimensions={0}, use_global_device_ids=true | all-gather | bytes 7680 | tf_op jit(solution)/shard_map/all_gather | solution.py:42
  146.8 1.3 constant_dynamic-update-slice_fusion.7
  148.1 1.3 constant_dynamic-update-slice_fusion.5
  149.5 1.3 constant_dynamic-update-slice_fusion.3
  151.1 2.5 constant_dynamic-slice_fusion
  153.6 31.9 %all-gather.14.cloned.1.call-done = bf16[1,1024,3072]{2,1,0:T(8,128)(2,1)} async-done(((bf16[1,512,3072]{2,1,0:T(8,128)(2,1)}), bf16[1,1024,3072]{2,1,0:T(8,128)(2,1)}) %all-gather.14.cloned.1.call-update) | async-done | bytes 6291472 | tf_op jit(solution)/shard_map/all_gather | solution.py:48
  185.5 83.5 %all-gather.16.cloned.1.call-done = bf16[4,512,3072]{2,1,0:T(8,128)(2,1)} async-done(((bf16[1,512,3072]{2,1,0:T(8,128)(2,1)}), bf16[4,512,3072]{2,1,0:T(8,128)(2,1)}) %all-gather.16.cloned.1.call-update) | async-done | bytes 12582928 | tf_op jit(solution)/shard_map/all_gather | solution.py:46
  269.0 19.4 %fusion.3 = f32[1024,2048]{0,1:T(8,128)} fusion(bf16[2048,3072]{1,0:T(8,128)(2,1)} %bitcast.40, bf16[1,1024,3072]{2,1,0:T(8,128)(2,1)} %all-gather.14.cloned.1.call-done, f32[3072]{0:T(1024)S(1)} %bitcast.38), kind=kOutput, calls=%fused_computation.5 | convolution fusion | flops 12894339072 | bytes 27275264 | tf_op jit(solution)/shard_map/dot_general | solution.py:26
  288.4 15.2 %all-gather.10.cloned.1.call-done = bf16[1,1024,1024]{2,1,0:T(8,128)(2,1)} async-done(((bf16[1,512,1024]{2,1,0:T(8,128)(2,1)}), bf16[1,1024,1024]{2,1,0:T(8,128)(2,1)}) %all-gather.10.cloned.1.call-update) | async-done | bytes 2097168 | tf_op jit(solution)/shard_map/all_gather | solution.py:48
  303.5 9.8 %fusion.1 = bf16[2048,1024]{1,0:T(8,128)(2,1)S(1)} fusion(f32[1024,2048]{0,1:T(8,128)} %fusion.3, bf16[2048,1024]{1,0:T(8,128)(2,1)} %bitcast.36, bf16[1,1024,1024]{2,1,0:T(8,128)(2,1)} %all-gather.10.cloned.1.call-done, f32[1024]{0:T(1024)S(1)} %bitcast.39), kind=kOutput, calls=%fused_computation.3 | convolution fusion | flops 4304404480 | bytes 18878464 | tf_op jit(solution)/shard_map/dot_general | solution.py:26
  313.4 3.2 copy.13
  316.6 97.4 %all_to_all.18 = bf16[1,4,512,1024]{3,1,0,2:T(4,128)(2,1)S(1)} all-to-all(bf16[1,4,512,1024]{3,1,0,2:T(4,128)(2,1)S(1)} %copy.13), channel_id=1, replica_groups=mesh['row'=2,'col'=4,'tm'=4] {'tm'}, dimensions={2} | all-to-all | bytes 8388608 | tf_op jit(solution)/shard_map/all_to_all | solution.py:61
  414.0 9.4 %convolution_bitcast_fusion = f32[4,4,128,1024]{3,0,2,1:T(4,128)S(1)} fusion(bf16[1,4,4,128,1024]{4,1,3,2,0:T(4,128)(2,1)S(1)} %bitcast.35, f32[4,4]{1,0:T(4,128)S(1)} %copy-done), kind=kOutput, calls=%fused_computation.7 | convolution fusion | flops 100663296 | bytes 12582976 | tf_op jit(solution)/shard_map/ft,tabc->fabc/dot_general | solution.py:58
  423.5 8.3 %copy.16 = f32[4,4,128,1024]{3,2,1,0:T(8,128)} copy(f32[4,4,128,1024]{3,0,2,1:T(4,128)S(1)} %convolution_bitcast_fusion) | data formatting | bytes 16777216 | tf_op jit(solution)/shard_map/ft,tabc->fabc/dot_general | solution.py:58
  (22 shorter events, 0.6 us)
Async XLA Ops:
  6.5 407.5 %copy-start = (f32[4,4]{1,0:T(4,128)S(1)}, f32[4,4]{1,0:T(4,128)}, u32[]{:S(2)}) copy-start(f32[4,4]{1,0:T(4,128)} %param.11) | copy-start | bytes 196
  6.5 68.6 %all-gather.12.cloned.1.call-start = ((), (), s32[]{:S(2)}) async-start(), calls=%async_computation.3 | async-start | bytes 3932160 | tf_op jit(solution)/shard_map/all_gather | solution.py:40
  7.3 98.0 %all-gather.8.cloned.1.call-start = ((), (), s32[]{:S(2)}) async-start(), calls=%async_computation.1 | async-start | bytes 1310720 | tf_op jit(solution)/shard_map/all_gather | solution.py:39
  8.0 177.5 %all-gather.14.cloned.1.call-start = ((), (), s32[]{:S(2)}) async-start(), calls=%async_computation.4 | async-start | bytes 9437184 | tf_op jit(solution)/shard_map/all_gather | solution.py:48
  75.1 193.9 %all-gather.16.cloned.1.call-start = ((), (), s32[]{:S(2)}) async-start(), calls=%async_computation.5 | async-start | bytes 15728640 | tf_op jit(solution)/shard_map/all_gather | solution.py:46
  75.7 227.8 %all-gather.10.cloned.1.call-start = ((), (), s32[]{:S(2)}) async-start(), calls=%async_computation.2 | async-start | bytes 3145728 | tf_op jit(solution)/shard_map/all_gather | solution.py:48
  105.3 45.6 %copy-start.1 = (bf16[1,512,1024]{2,1,0:T(8,128)(2,1)S(1)}, bf16[1,512,1024]{2,1,0:T(8,128)(2,1)}, u32[]{:S(2)}) copy-start(bf16[1,512,1024]{2,1,0:T(8,128)(2,1)} %all-gather.8.cloned.1.call-done) | copy-start | bytes 3145732
  105.3 14.4 %collective-permute-start = (bf16[1,512,1024]{2,1,0:T(8,128)(2,1)}, bf16[1,512,1024]{2,1,0:T(8,128)(2,1)S(1)}, u32[]{:S(2)}, u32[]{:S(2)}) collective-permute-start(bf16[1,512,1024]{2,1,0:T(8,128)(2,1)} %all-gather.8.cloned.1.call-done), channel_id=1, source_target_pairs={{0,4},{4,8},{8,12},{12,0},{1,5},{5,9},{9,13},{13,1},{2,6},{6,10},{... | collective-permute-start | bytes 3145736 | tf_op jit(solution)/shard_map/ppermute | solution.py:13
  119.7 27.1 %collective-permute-start.1 = (bf16[1,512,1024]{2,1,0:T(8,128)(2,1)S(1)}, bf16[1,512,1024]{2,1,0:T(8,128)(2,1)}, u32[]{:S(2)}, u32[]{:S(2)}) collective-permute-start(bf16[1,512,1024]{2,1,0:T(8,128)(2,1)S(1)} %collective-permute-done), channel_id=1, source_target_pairs={{0,4},{4,8},{8,12},{12,0},{1,5},{5,9},{9,13},{13,1},{2,6},{6,10},{... | collective-permute-start | bytes 3145736 | tf_op jit(solution)/shard_map/ppermute | solution.py:13
  119.7 29.7 %collective-permute-start.2 = (bf16[1,512,1024]{2,1,0:T(8,128)(2,1)}, bf16[1,512,1024]{2,1,0:T(8,128)(2,1)S(1)}, u32[]{:S(2)}, u32[]{:S(2)}) collective-permute-start(bf16[1,512,1024]{2,1,0:T(8,128)(2,1)} %all-gather.8.cloned.1.call-done), channel_id=1, source_target_pairs={{0,12},{4,0},{8,4},{12,8},{1,13},{5,1},{9,5},{13,9},{2,14},{6,2},{... | collective-permute-start | bytes 3145736 | tf_op jit(solution)/shard_map/ppermute | solution.py:15
Sparse Core Ops, SparseCore 0:
  8.9 66.1 all-gather.11
  76.7 28.5 all-gather.7
  106.8 78.6 all-gather.13
  186.9 82.0 all-gather.15
  270.4 33.0 all-gather.9
